TPU v7x, 32 devices: a whole 2x2x4 slice. The times are simulated.
32 devices in a mesh: space: 8 (over z, y), view: 4 (over x, core).
Axes of the slice: x: 2, y: 2, z: 4, core: 2. Of those that a mesh axis runs over, the one named last changes fastest.
Arguments:
- params: float32 [59, 16384], P(None, 'space'), may hold values from -8 to 514, as said below
- visible: int32 [8, 128, 16], P('space'), may hold values from 0 to 2047, as said below
- blocks: int32 [8, 128], P('space'), may hold values from 0 to 63, as said below
- counts: int32 [8, 8], P('space'), may hold values from 1 to 16
- depth_rank: int32 [4, 8], P('view'), may hold values from 0 to 7, each once within a row
- camera: float32 [4, 3], P('view'), may hold values from -0.006 to 0.006
- background: float32 [4, 3], P('view'), may hold values from 0 to 1
- target: float32 [4, 3, 128, 512], P('view', None, 'space'), may hold values from 0 to 1
Outputs:
- grad_params: float32 [59, 16384], P(None, 'space')
- rendered: float32 [4, 3, 128, 512], P('view', None, 'space')
- loss: float32 [4], P('view')
Inputs may be any that keep to these rules, and one draw needn't show every extreme that they name: `visible`: each row of a subspace's table lists 16 different splats of that subspace in increasing order; every splat of the subspace is listed exactly once. Slot j of a subspace goes to owner j // 16; the 16 slots that one subspace sends to one owner name different blocks. counts[s, o] live slots lead the 16 slots that subspace s sends to owner o. `params`: rows 6 to 9 of a column hold a quaternion whose first component lies in [1, 2].
All inputs are finite; a program needn't handle non-finite values.
Results may differ from a plain program's by a relative error of at most 0.0003.
Values sent between devices are 32-bit elements; how exact they have to be, the bound alone decides.
A program may use at most 64 MiB of HBM per device.

v0:
```python
import math

import jax
import jax.numpy as jnp
from jax import lax
from jax.sharding import PartitionSpec as P

HIGHEST = lax.Precision.HIGHEST
SH_ZERO = 0.28209479177387814
SH_ONE = 0.4886025119029199
SH_TWO = (
    1.0925484305920792,
    -1.0925484305920792,
    0.31539156525252005,
    -1.0925484305920792,
    0.5462742152960396,
)
SH_THREE = (
    -0.5900435899266435,
    2.890611442640554,
    -0.4570457994644658,
    0.3731763325901154,
    -0.4570457994644658,
    1.445305721320277,
    -0.5900435899266435,
)
DILATION = 0.3
SMOOTHING = 0.0001
SSIM_FIRST = 0.0001
SSIM_SECOND = 0.0009


def with_halo(x, sides, width):
    for axis, dim in sides:
        devices, length = (lax.axis_size(axis), x.shape[dim])
        up = [(i, (i + 1) % devices) for i in range(devices - 1)]
        down = [(j, i) for i, j in up]
        last = lax.slice_in_dim(x, length - width, length, axis=dim)
        first = lax.slice_in_dim(x, 0, width, axis=dim)
        before = lax.ppermute(last, axis, up)
        after = lax.ppermute(first, axis, down)
        x = jnp.concatenate([before, x, after], axis=dim)
    return x


def passed_along(x, axis, by):
    devices = lax.axis_size(axis)
    pairs = [(i, i + by) for i in range(devices) if 0 <= i + by < devices]
    return lax.ppermute(x, axis, pairs)


def camera_rotation(angles):
    cos_a, sin_a = (jnp.cos(angles[0]), jnp.sin(angles[0]))
    cos_b, sin_b = (jnp.cos(angles[1]), jnp.sin(angles[1]))
    cos_c, sin_c = (jnp.cos(angles[2]), jnp.sin(angles[2]))
    unity = jnp.ones_like(cos_a)
    nought = jnp.zeros_like(cos_a)
    turn_x = jnp.stack(
        [
            jnp.stack([unity, nought, nought]),
            jnp.stack([nought, cos_a, -sin_a]),
            jnp.stack([nought, sin_a, cos_a]),
        ]
    )
    turn_y = jnp.stack(
        [
            jnp.stack([cos_b, nought, sin_b]),
            jnp.stack([nought, unity, nought]),
            jnp.stack([-sin_b, nought, cos_b]),
        ]
    )
    turn_z = jnp.stack(
        [
            jnp.stack([cos_c, -sin_c, nought]),
            jnp.stack([sin_c, cos_c, nought]),
            jnp.stack([nought, nought, unity]),
        ]
    )
    return jnp.dot(jnp.dot(turn_z, turn_y, precision=HIGHEST), turn_x, precision=HIGHEST)


def harmonics(view_axis):
    axis_x, axis_y, axis_z = (view_axis[0], view_axis[1], view_axis[2])
    sq_x, sq_y, sq_z = (axis_x * axis_x, axis_y * axis_y, axis_z * axis_z)
    values = [
        SH_ZERO * jnp.ones_like(axis_x),
        -SH_ONE * axis_y,
        SH_ONE * axis_z,
        -SH_ONE * axis_x,
        SH_TWO[0] * axis_x * axis_y,
        SH_TWO[1] * axis_y * axis_z,
        SH_TWO[2] * (2.0 * sq_z - sq_x - sq_y),
        SH_TWO[3] * axis_x * axis_z,
        SH_TWO[4] * (sq_x - sq_y),
        SH_THREE[0] * axis_y * (3.0 * sq_x - sq_y),
        SH_THREE[1] * axis_x * axis_y * axis_z,
        SH_THREE[2] * axis_y * (4.0 * sq_z - sq_x - sq_y),
        SH_THREE[3] * axis_z * (2.0 * sq_z - 3.0 * sq_x - 3.0 * sq_y),
        SH_THREE[4] * axis_x * (4.0 * sq_z - sq_x - sq_y),
        SH_THREE[5] * axis_z * (sq_x - sq_y),
        SH_THREE[6] * axis_x * (sq_x - 3.0 * sq_y),
    ]
    return jnp.stack(values)


def project(param_in, angles, centre_x, centre_y):
    turn = camera_rotation(angles)
    scales = jnp.exp(param_in[3:6])
    quaternion = param_in[6:10]
    quaternion = quaternion / jnp.sqrt(jnp.sum(quaternion * quaternion, axis=0))
    part_w, part_x, part_y, part_z = (quaternion[0], quaternion[1], quaternion[2], quaternion[3])
    spin = [
        [
            1.0 - 2.0 * (part_y * part_y + part_z * part_z),
            2.0 * (part_x * part_y - part_w * part_z),
            2.0 * (part_x * part_z + part_w * part_y),
        ],
        [
            2.0 * (part_x * part_y + part_w * part_z),
            1.0 - 2.0 * (part_x * part_x + part_z * part_z),
            2.0 * (part_y * part_z - part_w * part_x),
        ],
        [
            2.0 * (part_x * part_z - part_w * part_y),
            2.0 * (part_y * part_z + part_w * part_x),
            1.0 - 2.0 * (part_x * part_x + part_y * part_y),
        ],
    ]
    frame = [
        [
            (
                turn[row, 0] * spin[0][col]
                + turn[row, 1] * spin[1][col]
                + turn[row, 2] * spin[2][col]
            )
            * scales[col]
            for col in range(3)
        ]
        for row in range(2)
    ]
    cov_xx = (
        frame[0][0] * frame[0][0] + frame[0][1] * frame[0][1] + frame[0][2] * frame[0][2] + DILATION
    )
    cov_xy = frame[0][0] * frame[1][0] + frame[0][1] * frame[1][1] + frame[0][2] * frame[1][2]
    cov_yy = (
        frame[1][0] * frame[1][0] + frame[1][1] * frame[1][1] + frame[1][2] * frame[1][2] + DILATION
    )
    determinant = cov_xx * cov_yy - cov_xy * cov_xy
    shift_x = param_in[0] - centre_x
    shift_y = param_in[1] - centre_y
    mean_u = turn[0, 0] * shift_x + turn[0, 1] * shift_y + turn[0, 2] * param_in[2] + centre_x
    mean_w = turn[1, 0] * shift_x + turn[1, 1] * shift_y + turn[1, 2] * param_in[2] + centre_y
    opacity = jax.nn.sigmoid(param_in[10])
    basis = harmonics(turn[2])
    coeffs = param_in[11:59].reshape(16, 3, param_in.shape[1])
    colour = 0.5 + jnp.sum(basis[:, None, None] * coeffs, axis=0)
    record = jnp.stack(
        [mean_u, mean_w, cov_yy / determinant, -cov_xy / determinant, cov_xx / determinant, opacity]
    )
    return jnp.concatenate([record, colour], axis=0)


def make_projector(view_angles, centre_x, centre_y):

    def apply(param_in):
        return project(param_in, view_angles, centre_x, centre_y)

    return apply


def render(gathered, grid_x, grid_y):
    delta_x = grid_x[:, None, :] - gathered[0][:, :, None]
    delta_y = grid_y[:, None, :] - gathered[1][:, :, None]
    powers = 0.5 * (
        gathered[2][:, :, None] * delta_x * delta_x
        + 2.0 * gathered[3][:, :, None] * delta_x * delta_y
        + gathered[4][:, :, None] * delta_y * delta_y
    )
    alphas = gathered[5][:, :, None] * jnp.exp(-powers)
    kept_log = jnp.log1p(-alphas)
    before = jnp.cumsum(kept_log, axis=1) - kept_log
    weights = alphas * jnp.exp(before)
    colour = jnp.einsum("skp,csk->scp", weights, gathered[6:9], precision=HIGHEST)
    return jnp.concatenate([colour, jnp.sum(kept_log, axis=1)[:, None, :]], axis=1)


def pixel_grid(owners, blocks_used, strip_rows, block_cols):
    inner = jnp.arange(128, dtype=jnp.int32)
    corner_y = owners * strip_rows + blocks_used // block_cols * 8
    corner_x = blocks_used % block_cols * 16
    grid_y = (corner_y[:, None] + inner[None, :] // 16).astype(jnp.float32) + 0.5
    grid_x = (corner_x[:, None] + inner[None, :] % 16).astype(jnp.float32) + 0.5
    return (grid_x, grid_y)


def composite(pieces, target_ids, depth_ranks, backdrop, block_rows, block_cols):
    block_count = block_rows * block_cols
    onehot = (
        target_ids[:, :, None] == jnp.arange(block_count, dtype=jnp.int32)[None, None, :]
    ).astype(jnp.float32)
    dense = jnp.einsum("scb,scqp->bsqp", onehot, pieces, precision=HIGHEST)
    kept_log = dense[:, :, 3]
    nearer = (depth_ranks[None, :] < depth_ranks[:, None]).astype(jnp.float32)
    before = jnp.einsum("st,btp->bsp", nearer, kept_log, precision=HIGHEST)
    picture = jnp.einsum("bsp,bscp->bcp", jnp.exp(before), dense[:, :, 0:3], precision=HIGHEST)
    picture = picture + backdrop[None, :, None] * jnp.exp(jnp.sum(kept_log, axis=1))[:, None, :]
    picture = picture.reshape(block_rows, block_cols, 3, 8, 16).transpose(2, 0, 3, 1, 4)
    return picture.reshape(3, block_rows * 8, block_cols * 16)


def blur_taps():
    raw_taps = [math.exp(-(offset - 5) * (offset - 5) / 4.5) for offset in range(11)]
    total = sum(raw_taps)
    return [value / total for value in raw_taps]


def blur(values, count):
    taps = blur_taps()
    width_px = values.shape[2]
    padded = jnp.pad(values, ((0, 0), (0, 0), (5, 5)))
    across = taps[0] * padded[:, :, 0:width_px]
    for offset in range(1, 11):
        across = across + taps[offset] * padded[:, :, offset : offset + width_px]
    result = taps[0] * across[:, 0:count]
    for offset in range(1, 11):
        result = result + taps[offset] * across[:, offset : offset + count]
    return result


def pixel_terms(picture, goal, count):
    mean_a = blur(picture, count)
    mean_b = blur(goal, count)
    var_a = blur(picture * picture, count) - mean_a * mean_a
    var_b = blur(goal * goal, count) - mean_b * mean_b
    cov_ab = blur(picture * goal, count) - mean_a * mean_b
    ssim = (
        (2.0 * mean_a * mean_b + SSIM_FIRST)
        * (2.0 * cov_ab + SSIM_SECOND)
        / ((mean_a * mean_a + mean_b * mean_b + SSIM_FIRST) * (var_a + var_b + SSIM_SECOND))
    )
    differ = picture[:, 5 : 5 + count] - goal[:, 5 : 5 + count]
    return 0.8 * jnp.sqrt(differ * differ + SMOOTHING) + 0.2 * (1.0 - ssim)


def shards(params, visible, blocks, counts, depth_rank, camera, background, target):
    devices = lax.axis_size("space")
    me_index = lax.axis_index("space")
    slot_total = visible.shape[1]
    list_length = visible.shape[2]
    capacity = slot_total // devices
    strip_rows = target.shape[2]
    width_px = target.shape[3]
    block_rows = strip_rows // 8
    block_cols = width_px // 16
    height_px = strip_rows * devices
    lists = visible[0]
    slot_blocks = blocks[0]
    live = jnp.arange(capacity, dtype=jnp.int32)[None, :] < counts[0][:, None]
    target_ids = jnp.where(live, slot_blocks.reshape(devices, capacity), -1)
    centre_x = 0.5 * width_px
    centre_y = 0.5 * height_px
    records, pull_project = jax.vjp(make_projector(camera[0], centre_x, centre_y), params)

    def sender_side(record_in):
        picked = record_in[:, lists]
        return picked.reshape(9, devices, capacity * list_length).transpose(1, 0, 2)

    message, pull_sender = jax.vjp(sender_side, records)
    received, recv_ids = (
        lax.all_to_all(message, "space", split_axis=0, concat_axis=0, tiled=True),
        lax.all_to_all(target_ids, "space", split_axis=0, concat_axis=0, tiled=True),
    )
    own_blocks = jnp.maximum(recv_ids.reshape(devices * capacity), 0)
    grid_x, grid_y = pixel_grid(
        jnp.full(own_blocks.shape, me_index, jnp.int32), own_blocks, strip_rows, block_cols
    )

    def owner_side(recv_in):
        gathered = (
            recv_in.reshape(devices, 9, capacity, list_length)
            .transpose(1, 0, 2, 3)
            .reshape(9, devices * capacity, list_length)
        )
        pieces = render(gathered, grid_x, grid_y).reshape(devices, capacity, 4, 128)
        return composite(pieces, recv_ids, depth_rank[0], background[0], block_rows, block_cols)

    strip, pull_owner = jax.vjp(owner_side, received)
    stacked = jnp.concatenate([strip, target[0]], axis=0)
    extended = with_halo(stacked, (("space", 1),), 5)
    goal = extended[3:6]

    def local_sum(picture):
        return jnp.sum(pixel_terms(picture, goal, strip_rows))

    own_loss, pull_terms = jax.vjp(local_sum, extended[0:3])
    grad_extended = pull_terms(jnp.ones((), jnp.float32))[0]
    from_below = passed_along(grad_extended[:, 0:5], "space", -1)
    from_above = passed_along(grad_extended[:, strip_rows + 5 : strip_rows + 10], "space", 1)
    grad_strip = grad_extended[:, 5 : strip_rows + 5]
    grad_strip = grad_strip.at[:, strip_rows - 5 :].add(from_below).at[:, 0:5].add(from_above)
    grad_received = pull_owner(grad_strip)[0]
    returned = lax.all_to_all(grad_received, "space", split_axis=0, concat_axis=0, tiled=True)
    grad_records = pull_sender(returned)[0]
    grad_params = lax.psum(pull_project(grad_records)[0], "view")
    loss_sum = lax.psum(own_loss, "space")
    loss_value = (loss_sum / (3.0 * height_px * width_px)).reshape(1)
    return (grad_params, strip[None], loss_value)


def solution(mesh):
    in_specs = (
        P(None, "space"),
        P("space", None, None),
        P("space", None),
        P("space", None),
        P("view", None),
        P("view", None),
        P("view", None),
        P("view", None, "space", None),
    )
    out_specs = (P(None, "space"), P("view", None, "space", None), P("view"))
    return jax.shard_map(shards, mesh=mesh, in_specs=in_specs, out_specs=out_specs, check_vma=False)
```

profile of v0, /device:TPU:0, one launch (start us, length us, event | category | flops | bytes accessed | tf_op | source)
XLA Modules:
  0.0 244.3 jit_solution(11177102204411708343)
XLA Ops:
  9.9 7.3 %all-to-all-start = ((s32[8,1,16]{2,1,0:T(1,128)}), s32[8,1,16]{2,1,0:T(1,128)S(1)}, u32[]{:S(2)}, u32[]{:S(2)}) async-start(s32[8,1,16]{2,1,0:T(1,128)} %bitcast.45), calls=%async_computation | async-start | bytes 8192 | tf_op jit(solution)/shard_map/all_to_all | solution.py:271
  37.9 0.9 multiply_reduce_fusion.6
  38.9 4.8 %add_divide_fusion = (f32[1,2048]{1,0:T(1,128)S(1)}, f32[1,2048]{1,0:T(1,128)S(1)}, f32[1,2048]{1,0:T(1,128)S(1)}) fusion(f32[59,2048]{1,0:T(8,128)} %param.12, f32[]{:T(128)} %bitcast.50, f32[]{:T(128)} %bitcast.49, f32[]{:T(128)} %bitcast.48, f32[]{:T(128)} %bitcast.53, f32[]{:T(128)} %bitcast.52, f32[]{:T(128)} %bitcast.51), kind=kLoop, calls=%fused_computation.484 | loop fusion | flops 34816 | bytes 57368 | tf_op jit(solution)/shard_map/jvp()/div | solution.py:153
  44.6 1.1 slice.579
  52.8 0.9 slice_divide_fusion
  55.5 4.6 %fusion.269 = (f32[1,2048]{1,0:T(1,128)S(1)}, f32[1,2048]{1,0:T(1,128)S(1)}, f32[1,2048]{1,0:T(1,128)}, f32[1,2048]{1,0:T(1,128)S(1)}, f32[1,2048]{1,0:T(1,128)}...) fusion(f32[3,2048]{1,0:T(4,128)S(1)} %slice_exponential_fusion,, ...), kind=kLoop, calls=%fused_computation.586 | loop fusion | flops 159744 | bytes 213040 | tf_op jit(solution)/shard_map/jvp()/div | solution.py:158
  61.3 5.5 %gather_fusion = f32[2048,9]{1,0:T(8,128)S(1)} fusion(f32[9,2048]{0,1:T(8,128)S(1)} %copy.299, s32[2048]{0:T(1024)S(1)} %broadcast_clamp_fusion), kind=kCustom, calls=%fused_computation | custom fusion | bytes 155648 | tf_op jit(solution)/shard_map/jvp()/gather | solution.py:265
  66.8 0.9 copy.300
  68.6 6.0 %all-to-all-start.1 = ((f32[8,9,256]{2,1,0:T(8,128)}), f32[8,9,256]{2,1,0:T(8,128)S(1)}, u32[]{:S(2)}, u32[]{:S(2)}) async-start(f32[8,9,256]{2,1,0:T(8,128)} %copy.301), calls=%async_computation.1 | async-start | bytes 262144 | tf_op jit(solution)/shard_map/all_to_all | solution.py:270
  75.1 6.9 %all-to-all-done.1 = f32[8,9,256]{2,1,0:T(8,128)S(1)} async-done(((f32[8,9,256]{2,1,0:T(8,128)}), f32[8,9,256]{2,1,0:T(8,128)S(1)}, u32[]{:S(2)}, u32[]{:S(2)}) %all-to-all-start.1) | async-done | bytes 73760 | tf_op jit(solution)/shard_map/all_to_all | solution.py:270
  82.5 1.7 negate_log-plus-one_fusion
  84.6 3.7 %fusion.30 = f32[128,3,128]{2,1,0:T(4,128)S(1)} fusion(f32[3,128,16]{2,0,1:T(4,128)S(1)} %bitcast.204, f32[128,16]{1,0:T(8,128)S(1)} %bitcast.169, f32[128,16,128]{2,0,1:T(8,128)S(1)} %fusion.26, f32[128,16]{1,0:T(8,128)S(1)} %bitcast.174, f32[128,16]{1,0:T(8,128)S(1)} %bitcast.179, f32[128,128]{1,0:T(8,128)S(1)} %get-tuple-element.200, ...), kind=kOutput, calls=%fused_computation.64 | convolution fusion | flops 13631488 | bytes 1449984 | tf_op jit(solution)/shard_map/jvp(skp,csk->scp)/dot_general | solution.py:183
  93.5 2.1 collective-permute-start
  95.6 1.5 collective-permute-start.1
  97.1 1.6 collective-permute-done
  98.8 3.3 %collective-permute-done.1 = f32[6,5,512]{2,1,0:T(8,128)S(1)} collective-permute-done((f32[6,5,512]{2,1,0:T(8,128)S(1)}, f32[6,5,512]{2,1,0:T(8,128)S(1)}, u32[]{:S(2)}, u32[]{:S(2)}) %collective-permute-start.1) | collective-permute-done | bytes 61472 | tf_op jit(solution)/shard_map/ppermute | solution.py:41
  105.2 1.3 add_reduce_fusion
  108.7 1.0 fusion.41
  109.8 1.3 collective-permute-start.2
  111.1 4.8 %collective-permute-start.3 = (f32[3,5,512]{2,1,0:T(8,128)S(1)}, f32[3,5,512]{2,1,0:T(8,128)S(1)}, u32[]{:S(2)}, u32[]{:S(2)}) collective-permute-start(f32[3,5,512]{2,1,0:T(8,128)S(1)} %get-tuple-element.131), channel_id=1, source_target_pairs={{0,4},{4,8},{8,12},{12,16},{16,20},{20,24},{24,28},{1,5},{5,9},{9,... | collective-permute-start | bytes 92168 | tf_op jit(solution)/shard_map/ppermute | solution.py:49
  116.1 1.3 collective-permute-done.3
  119.6 0.9 copy-done.6
  124.2 4.2 %convolution_bitcast_fusion.1 = f32[3,128,16]{2,0,1:T(4,128)S(1)} fusion(f32[128,16]{1,0:T(8,128)S(1)} %bitcast.170, f32[128,16,128]{2,0,1:T(8,128)S(1)} %copy-done.3, f32[128,3,128]{2,0,1:T(8,128)S(1)} %split.13, f32[128,16]{1,0:T(8,128)S(1)} %bitcast.175, f32[128,16]{1,0:T(8,128)S(1)} %bitcast.180, f32[128,128]{1,0:T(8,128)S(1)} %copy-done.18, ...), kind=kOutput, calls=%fused_computation.18 | convolution fusion | flops 13631488 | bytes 1449984 | tf_op jit(solution)/shard_map/transpose(jvp(skp,csk->scp))/dot_general | solution.py:183
  128.4 4.0 %multiply_multiply_fusion = (f32[128,16,128]{2,1,0:T(8,128)S(1)}, f32[128,16,128]{2,1,0:T(8,128)S(1)}) fusion(f32[128,16]{1,0:T(8,128)S(1)} %bitcast.171, f32[128,16,128]{2,0,1:T(8,128)S(1)} %copy-done.3, f32[128,16]{1,0:T(8,128)S(1)} %bitcast.176, f32[128,16]{1,0:T(8,128)S(1)} %bitcast.181, f32[128,128]{1,0:T(8,128)S(1)} %copy-done.18, ...), kind=kOutput, calls=%fused_computation.50 | convolution fusion | flops 13893632 | bytes 3547136 | tf_op jit(solution)/shard_map/transpose(jvp(skp,csk->scp))/dot_general | solution.py:183
  132.7 5.5 %fusion.15 = (f32[128,16]{1,0:T(8,128)S(1)}, f32[128,16]{1,0:T(8,128)S(1)}, f32[128,16]{1,0:T(8,128)S(1)}, f32[128,16]{1,0:T(8,128)S(1)}, f32[128,16]{1,0:T(8,128)S(1)}, /*index=5*/f32[128,16]{1,0:T(8,128)S(1)}) fusion(f32[128,16]{1,0:T(8,128)S(1)} %bitcast.182, f32[128,128]{1,0:T(8,128)S(1)} %copy-done.18, f32[128,16]{1,0:T(8,128)S(1)} %bitcast.177, ...), kind=kLoop, calls=%fused_computation.32 | loop fusion | flops 13357056 | bytes 3440640 | tf_op jit(solution)/shard_map/transpose(jvp())/reduce_sum | solution.py:177
  140.3 6.8 %all-to-all-start.2 = ((f32[8,9,256]{2,1,0:T(8,128)}), f32[8,9,256]{2,1,0:T(8,128)S(1)}, u32[]{:S(2)}, u32[]{:S(2)}) async-start(f32[8,9,256]{2,1,0:T(8,128)} %copy.321), calls=%async_computation.2 | async-start | bytes 262144 | tf_op jit(solution)/shard_map/all_to_all | solution.py:302
  147.8 6.6 %all-to-all-done.2 = f32[8,9,256]{2,1,0:T(8,128)S(1)} async-done(((f32[8,9,256]{2,1,0:T(8,128)}), f32[8,9,256]{2,1,0:T(8,128)S(1)}, u32[]{:S(2)}, u32[]{:S(2)}) %all-to-all-start.2) | async-done | bytes 73760 | tf_op jit(solution)/shard_map/all_to_all | solution.py:302
  154.7 1.8 copy.352
  156.5 12.3 %scatter_custom_fusion = f32[9,2048]{0,1:T(8,128)S(1)} fusion(s32[2048]{0:T(1024)} %copy-done.36, f32[2048,9]{1,0:T(8,128)} %bitcast.166, f32[]{:T(128)} %constant.222.clone.1), kind=kCustom, calls=%fused_computation.61 | custom fusion | flops 18432 | bytes 74240 | tf_op jit(solution)/shard_map/transpose(jvp())/scatter-add | solution.py:265
  168.8 1.3 split.15
  170.2 3.7 %fusion.270 = (f32[1,2048]{0,1:T(8,128)}, f32[1,2048]{0,1:T(8,128)}, f32[1,2048]{0,1:T(8,128)}, f32[1,2048]{0,1:T(8,128)}, f32[1,2048]{0,1:T(8,128)S(1)}, /*index=5*/f32[1,2048]{0,1:T(8,128)}) fusion(f32[9,2048]{0,1:T(8,128)S(1)} %scatter_custom_fusion), kind=kLoop, calls=%fused_computation.587 | loop fusion | bytes 98304 | tf_op jit(solution)/shard_map/transpose(jvp())/unstack | solution.py:157
  173.9 1.6 copy.324
  175.5 0.9 broadcast_in_dim.33
  176.5 1.6 copy.354
  178.4 1.7 copy.359
  180.1 1.6 copy.357
  183.2 4.0 %add_add_fusion.6 = (f32[1,2048]{1,0:T(1,128)S(1)}, f32[1,2048]{1,0:T(1,128)S(1)}, f32[1,2048]{1,0:T(1,128)S(1)}, f32[1,2048]{1,0:T(1,128)S(1)}, f32[1,2048]{1,0...) fusion(f32[4,2048]{1,0:T(4,128)S(1)} %slice_divide_fusion, ...), kind=kLoop, calls=%fused_computation.445 | loop fusion | flops 167936 | bytes 237592 | tf_op jit(solution)/shard_map/transpose(jvp())/add_any | solution.py:114
  187.3 2.5 %multiply_add_fusion.8 = f32[1,2048]{1,0:T(1,128)S(1)} fusion(f32[1,2048]{1,0:T(1,128)S(1)} %get-tuple-element.62, f32[1,2048]{1,0:T(1,128)S(1)} %get-tuple-element.67, f32[1,2048]{1,0:T(1,128)S(1)} %get-tuple-element.66, f32[1,2048]{1,0:T(1,128)S(1)} %get-tuple-element.63, f32[1,2048]{1,0:T(1,128)S(1)} %get-tuple-element.65, ...), kind=kLoop, calls=%fused_computation.469 | loop fusion | flops 65536 | bytes 139280 | tf_op jit(solution)/shard_map/transpose(jvp())/add_any | solution.py:115
  189.9 2.7 %add_add_fusion.5 = f32[1,2048]{1,0:T(1,128)S(1)} fusion(f32[1,2048]{1,0:T(1,128)S(1)} %get-tuple-element.62, f32[1,2048]{1,0:T(1,128)S(1)} %get-tuple-element.67, f32[1,2048]{1,0:T(1,128)S(1)} %get-tuple-element.66, f32[1,2048]{1,0:T(1,128)S(1)} %get-tuple-element.64, f32[1,2048]{1,0:T(1,128)S(1)} %get-tuple-element.65, ...), kind=kLoop, calls=%fused_computation.444 | loop fusion | flops 65536 | bytes 139280 | tf_op jit(solution)/shard_map/transpose(jvp())/add_any | solution.py:114
  194.7 1.0 multiply_reduce_fusion.5
  196.4 1.0 add_add_fusion.3
  197.5 3.8 %multiply_add_fusion.12 = (f32[1,2048]{1,0:T(1,128)S(1)}, f32[1,2048]{1,0:T(1,128)S(1)}, f32[1,2048]{1,0:T(1,128)S(1)}, f32[1,2048]{1,0:T(1,128)S(1)}) fusion(f32[1,2048]{1,0:T(1,128)S(1)} %copy.356, f32[1,2048]{1,0:T(1,128)S(1)} %copy.355, f32[]{:T(128)} %bitcast.52, f32[]{:T(128)} %bitcast.49, f32[]{:T(128)} %bitcast.48, f32[]{:T(128)} %bitcast.51, ...), kind=kLoop, calls=%fused_computation.483 | loop fusion | flops 16384 | bytes 49176 | tf_op jit(solution)/shard_map/transpose(jvp())/add_any | solution.py:151
  201.3 0.9 add_multiply_fusion.1
  202.2 0.9 pad_add_fusion.1
  203.1 1.0 reshape.522
  204.2 18.8 %psum.15 = f32[]{:T(128)} all-reduce(f32[]{:T(128)} %get-tuple-element.56), channel_id=1, replica_groups=mesh['space'=8,'view'=4] {'space'}, use_global_device_ids=true, to_apply=%region_17.18 | all-reduce | flops 1 | bytes 8 | tf_op jit(solution)/shard_map/psum | solution.py:305
  223.6 10.8 %all-reduce.101.cloned.1.call-done = f32[59,2048]{1,0:T(8,128)} async-done(((f32[59,2048]{1,0:T(8,128)}), f32[59,2048]{1,0:T(8,128)}) %all-reduce.101.cloned.1.call-update) | async-done | bytes 483344 | tf_op jit(solution)/shard_map/psum | solution.py:304
  234.4 1.9 copy.406
  (255 shorter events, 37.6 us)
Async XLA Ops:
  9.9 58.7 %all-to-all-start = ((s32[8,1,16]{2,1,0:T(1,128)}), s32[8,1,16]{2,1,0:T(1,128)S(1)}, u32[]{:S(2)}, u32[]{:S(2)}) async-start(s32[8,1,16]{2,1,0:T(1,128)} %bitcast.45), calls=%async_computation | async-start | bytes 8192 | tf_op jit(solution)/shard_map/all_to_all | solution.py:271
  38.9 13.3 %copy-start.31 = (f32[2048]{0:T(1024)}, f32[2048]{0:T(1024)S(1)}, u32[]{:S(2)}) copy-start(f32[2048]{0:T(1024)S(1)} %multiply_reduce_fusion.6) | copy-start | bytes 24580
  43.7 17.0 %copy-start.33 = (f32[1,2048]{1,0:T(1,128)}, f32[1,2048]{1,0:T(1,128)S(1)}, u32[]{:S(2)}) copy-start(f32[1,2048]{1,0:T(1,128)S(1)} %get-tuple-element.121) | copy-start | bytes 24580
  50.8 1.3 copy-start.52
  52.8 0.9 copy-start.29
  68.6 19.8 %copy-start.27 = (s32[8,1,16]{2,1,0:T(1,128)}, s32[8,1,16]{2,1,0:T(1,128)S(1)}, u32[]{:S(2)}) copy-start(s32[8,1,16]{2,1,0:T(1,128)S(1)} %all-to-all-done) | copy-start | bytes 1540
  68.6 13.3 %all-to-all-start.1 = ((f32[8,9,256]{2,1,0:T(8,128)}), f32[8,9,256]{2,1,0:T(8,128)S(1)}, u32[]{:S(2)}, u32[]{:S(2)}) async-start(f32[8,9,256]{2,1,0:T(8,128)} %copy.301), calls=%async_computation.1 | async-start | bytes 262144 | tf_op jit(solution)/shard_map/all_to_all | solution.py:270
  75.0 9.5 %copy-start.17 = (f32[128,128]{1,0:T(8,128)}, f32[128,128]{1,0:T(8,128)S(1)}, u32[]{:S(2)}) copy-start(f32[128,128]{1,0:T(8,128)S(1)} %get-tuple-element.200) | copy-start | bytes 196612
  75.0 9.5 %copy-start.19 = (f32[128,128]{1,0:T(8,128)}, f32[128,128]{1,0:T(8,128)S(1)}, u32[]{:S(2)}) copy-start(f32[128,128]{1,0:T(8,128)S(1)} %get-tuple-element.201) | copy-start | bytes 196612
  82.3 2.3 copy-start.7
  82.3 2.3 copy-start.9
  82.3 2.3 copy-start.11
  82.3 2.3 copy-start.13
  82.3 2.3 copy-start.15
  82.5 2.2 copy-start.23
  84.5 3.8 %copy-start.2 = (f32[128,16,128]{2,0,1:T(8,128)}, f32[128,16,128]{2,0,1:T(8,128)S(1)}, u32[]{:S(2)}) copy-start(f32[128,16,128]{2,0,1:T(8,128)S(1)} %fusion.26) | copy-start | bytes 3145732
  92.6 0.9 copy-start.5
  93.5 5.3 %collective-permute-start = (f32[6,5,512]{2,1,0:T(8,128)S(1)}, f32[6,5,512]{2,1,0:T(8,128)S(1)}, u32[]{:S(2)}, u32[]{:S(2)}) collective-permute-start(f32[6,5,512]{2,1,0:T(8,128)S(1)} %get-tuple-element.148), channel_id=1, source_target_pairs={{0,4},{4,8},{8,12},{12,16},{16,20},{20,24},{24,28},{1,5},{5,9},{9,... | collective-permute-start | bytes 184328 | tf_op jit(solution)/shard_map/ppermute | solution.py:40
  95.6 6.5 %collective-permute-start.1 = (f32[6,5,512]{2,1,0:T(8,128)S(1)}, f32[6,5,512]{2,1,0:T(8,128)S(1)}, u32[]{:S(2)}, u32[]{:S(2)}) collective-permute-start(f32[6,5,512]{2,1,0:T(8,128)S(1)} %get-tuple-element.149), channel_id=1, source_target_pairs={{4,0},{8,4},{12,8},{16,12},{20,16},{24,20},{28,24},{5,1},{9,5},{13... | collective-permute-start | bytes 184328 | tf_op jit(solution)/shard_map/ppermute | solution.py:41
  109.8 6.1 %collective-permute-start.2 = (f32[3,5,512]{2,1,0:T(8,128)S(1)}, f32[3,5,512]{2,1,0:T(8,128)S(1)}, u32[]{:S(2)}, u32[]{:S(2)}) collective-permute-start(f32[3,5,512]{2,1,0:T(8,128)S(1)} %get-tuple-element.132), channel_id=1, source_target_pairs={{4,0},{8,4},{12,8},{16,12},{20,16},{24,20},{28,24},{5,1},{9,5},{13... | collective-permute-start | bytes 92168 | tf_op jit(solution)/shard_map/ppermute | solution.py:49
  111.1 6.3 %collective-permute-start.3 = (f32[3,5,512]{2,1,0:T(8,128)S(1)}, f32[3,5,512]{2,1,0:T(8,128)S(1)}, u32[]{:S(2)}, u32[]{:S(2)}) collective-permute-start(f32[3,5,512]{2,1,0:T(8,128)S(1)} %get-tuple-element.131), channel_id=1, source_target_pairs={{0,4},{4,8},{8,12},{12,16},{16,20},{20,24},{24,28},{1,5},{5,9},{9,... | collective-permute-start | bytes 92168 | tf_op jit(solution)/shard_map/ppermute | solution.py:49
  119.5 1.0 copy-start.6
  120.4 1.1 copy-start.51
  120.7 0.8 copy-start.22
  122.6 1.2 copy-start.3
  122.6 1.2 copy-start.20
  123.2 0.9 copy-start.8
  123.2 0.9 copy-start.10
  123.2 0.9 copy-start.12
  123.2 1.0 copy-start.14
  123.2 1.0 copy-start.16
  123.2 1.0 copy-start.18
  124.2 4.2 %copy-start.24 = (f32[3,8,16,16]{3,0,2,1:T(4,128)S(1)}, f32[3,8,16,16]{3,0,2,1:T(4,128)}, u32[]{:S(2)}) copy-start(f32[3,8,16,16]{3,0,2,1:T(4,128)} %copy-done.23) | copy-start | bytes 73732
  140.3 6.8 %copy-start.54 = (f32[16]{0:T(128)S(1)}, f32[16]{0:T(128)}, u32[]{:S(2)}) copy-start(f32[16]{0:T(128)} %copy-done.53) | copy-start | bytes 196
  140.3 14.1 %all-to-all-start.2 = ((f32[8,9,256]{2,1,0:T(8,128)}), f32[8,9,256]{2,1,0:T(8,128)S(1)}, u32[]{:S(2)}, u32[]{:S(2)}) async-start(f32[8,9,256]{2,1,0:T(8,128)} %copy.321), calls=%async_computation.2 | async-start | bytes 262144 | tf_op jit(solution)/shard_map/all_to_all | solution.py:302
  147.1 87.4 %all-reduce.101.cloned.1.call-start = ((), (), s32[]{:S(2)}) async-start(), calls=%async_computation.3 | async-start | bytes 1048576 | tf_op jit(solution)/shard_map/psum | solution.py:304
  175.5 2.6 %copy-start.1 = (f32[1,2048]{0,1:T(8,128)S(1)}, f32[1,2048]{0,1:T(8,128)}, u32[]{:S(2)}) copy-start(f32[1,2048]{0,1:T(8,128)} %get-tuple-element.106) | copy-start | bytes 24580
  176.5 1.6 copy-start.34
  178.4 3.4 %copy-start = (f32[1,2048]{0,1:T(8,128)S(1)}, f32[1,2048]{0,1:T(8,128)}, u32[]{:S(2)}) copy-start(f32[1,2048]{0,1:T(8,128)} %get-tuple-element.108) | copy-start | bytes 24580
  180.1 1.6 copy-start.26
  180.1 1.6 copy-start.43
  182.2 5.1 %copy-start.42 = (f32[1,2048]{1,0:T(1,128)S(1)}, f32[1,2048]{1,0:T(1,128)}, u32[]{:S(2)}) copy-start(f32[1,2048]{1,0:T(1,128)} %get-tuple-element.100) | copy-start | bytes 24580
  182.2 5.1 %copy-start.41 = (f32[1,2048]{1,0:T(1,128)S(1)}, f32[1,2048]{1,0:T(1,128)}, u32[]{:S(2)}) copy-start(f32[1,2048]{1,0:T(1,128)} %get-tuple-element.102) | copy-start | bytes 24580
  182.2 7.7 %copy-start.40 = (f32[1,2048]{1,0:T(1,128)S(1)}, f32[1,2048]{1,0:T(1,128)}, u32[]{:S(2)}) copy-start(f32[1,2048]{1,0:T(1,128)} %get-tuple-element.95) | copy-start | bytes 24580
  187.2 10.1 %copy-start.4 = (f32[48,2048]{1,0:T(8,128)S(1)}, f32[48,2048]{1,0:T(8,128)}, u32[]{:S(2)}) copy-start(f32[48,2048]{1,0:T(8,128)} %broadcast_in_dim.33) | copy-start | bytes 1179652
  189.9 2.7 %copy-start.39 = (f32[1,2048]{1,0:T(1,128)S(1)}, f32[1,2048]{1,0:T(1,128)}, u32[]{:S(2)}) copy-start(f32[1,2048]{1,0:T(1,128)} %get-tuple-element.98) | copy-start | bytes 24580
  194.7 1.0 copy-start.32
  196.4 1.0 copy-start.57
  (23 other events, 15.4 us)
Sparse Core Ops, SparseCore 0:
  203.2 31.1 all-reduce.100
where the time goes:
time: 246 us; the launch traced here: 244 us
  other arithmetic  61 us (25%)
  local copies, waits for them, and re-layouts  49.4 us (20%)
  between operations  40.5 us (16%)
  waiting for transfers between devices  30.6 us (12%)
  starting transfers between devices  29.8 us (12%)
  blocking collectives  18.8 us (8%)
  matrix products  14.2 us (6%)
    unnamed x135, local copies, waits for them, and re-layouts  21.7 us
    psum x1, blocking collectives, shards(): loss_sum = lax.psum(own_loss, 'space')  18.8 us
    scatter-add x1, other arithmetic, sender_side(): picked = record_in[:, lists]  12.3 us
    dot_general x3, matrix products, render(): jnp.einsum('skp,csk->scp', weights, gathered[6:9], precision=HIGHEST)  11.8 us
    psum x1, waiting for transfers between devices, shards(): grad_params = lax.psum(pull_project(grad_records)[0], 'view')  10.8 us
    all_to_all x1, starting transfers between devices, shards(): lax.all_to_all(target_ids, 'space', split_axis=0, concat_axis=0, tiled=True)  7.31 us
    all_to_all x1, waiting for transfers between devices, shards(): lax.all_to_all(message, 'space', split_axis=0, concat_axis=0, tiled=True)  6.88 us
    all_to_all x1, starting transfers between devices, shards(): lax.all_to_all(grad_received, 'space', split_axis=0, concat_axis=0, tiled...  6.79 us
  transfers between devices with their start and end apart: 8, of which 6 were waited for; matrix products, arithmetic and copies ran while one was open for 11% of the time, Pallas kernels for 0%

commit v1 on v0

--- a/solution.py
+++ b/solution.py
@@ -1,8 +1,11 @@
+import functools
 import math
 
 import jax
 import jax.numpy as jnp
 from jax import lax
+from jax.experimental import pallas as pl
+from jax.experimental.pallas import tpu as pltpu
 from jax.sharding import PartitionSpec as P
 
 HIGHEST = lax.Precision.HIGHEST
@@ -43,46 +46,21 @@
     return x
 
 
-def passed_along(x, axis, by):
-    devices = lax.axis_size(axis)
-    pairs = [(i, i + by) for i in range(devices) if 0 <= i + by < devices]
-    return lax.ppermute(x, axis, pairs)
-
-
 def camera_rotation(angles):
     cos_a, sin_a = (jnp.cos(angles[0]), jnp.sin(angles[0]))
     cos_b, sin_b = (jnp.cos(angles[1]), jnp.sin(angles[1]))
     cos_c, sin_c = (jnp.cos(angles[2]), jnp.sin(angles[2]))
-    unity = jnp.ones_like(cos_a)
-    nought = jnp.zeros_like(cos_a)
-    turn_x = jnp.stack(
-        [
-            jnp.stack([unity, nought, nought]),
-            jnp.stack([nought, cos_a, -sin_a]),
-            jnp.stack([nought, sin_a, cos_a]),
-        ]
-    )
-    turn_y = jnp.stack(
-        [
-            jnp.stack([cos_b, nought, sin_b]),
-            jnp.stack([nought, unity, nought]),
-            jnp.stack([-sin_b, nought, cos_b]),
-        ]
-    )
-    turn_z = jnp.stack(
-        [
-            jnp.stack([cos_c, -sin_c, nought]),
-            jnp.stack([sin_c, cos_c, nought]),
-            jnp.stack([nought, nought, unity]),
-        ]
-    )
-    return jnp.dot(jnp.dot(turn_z, turn_y, precision=HIGHEST), turn_x, precision=HIGHEST)
+    return [
+        [cos_c * cos_b, cos_c * sin_b * sin_a - sin_c * cos_a, cos_c * sin_b * cos_a + sin_c * sin_a],
+        [sin_c * cos_b, sin_c * sin_b * sin_a + cos_c * cos_a, sin_c * sin_b * cos_a - cos_c * sin_a],
+        [-sin_b, cos_b * sin_a, cos_b * cos_a],
+    ]
 
 
 def harmonics(view_axis):
     axis_x, axis_y, axis_z = (view_axis[0], view_axis[1], view_axis[2])
     sq_x, sq_y, sq_z = (axis_x * axis_x, axis_y * axis_y, axis_z * axis_z)
-    values = [
+    return [
         SH_ZERO * jnp.ones_like(axis_x),
         -SH_ONE * axis_y,
         SH_ONE * axis_z,
@@ -100,15 +78,13 @@
         SH_THREE[5] * axis_z * (sq_x - sq_y),
         SH_THREE[6] * axis_x * (sq_x - 3.0 * sq_y),
     ]
-    return jnp.stack(values)
-
-
-def project(param_in, angles, centre_x, centre_y):
-    turn = camera_rotation(angles)
-    scales = jnp.exp(param_in[3:6])
-    quaternion = param_in[6:10]
-    quaternion = quaternion / jnp.sqrt(jnp.sum(quaternion * quaternion, axis=0))
-    part_w, part_x, part_y, part_z = (quaternion[0], quaternion[1], quaternion[2], quaternion[3])
+
+
+def geometry(rows, turns, centre_x, centre_y):
+    scales = [jnp.exp(rows[i]) for i in range(3, 6)]
+    quat = rows[6:10]
+    length = jnp.sqrt(quat[0] * quat[0] + quat[1] * quat[1] + quat[2] * quat[2] + quat[3] * quat[3])
+    part_w, part_x, part_y, part_z = [q / length for q in quat]
     spin = [
         [
             1.0 - 2.0 * (part_y * part_y + part_z * part_z),
@@ -126,46 +102,130 @@
             1.0 - 2.0 * (part_x * part_x + part_y * part_y),
         ],
     ]
-    frame = [
-        [
-            (
-                turn[row, 0] * spin[0][col]
-                + turn[row, 1] * spin[1][col]
-                + turn[row, 2] * spin[2][col]
-            )
-            * scales[col]
-            for col in range(3)
+    local = [[spin[r][c] * scales[c] for c in range(3)] for r in range(3)]
+    opacity = 1.0 / (1.0 + jnp.exp(-rows[10]))
+    shift_x = rows[0] - centre_x
+    shift_y = rows[1] - centre_y
+    records = []
+    for turn in turns:
+        frame = [
+            [
+                turn[r][0] * local[0][c] + turn[r][1] * local[1][c] + turn[r][2] * local[2][c]
+                for c in range(3)
+            ]
+            for r in range(2)
         ]
-        for row in range(2)
+        cov_xx = sum(frame[0][c] * frame[0][c] for c in range(3)) + DILATION
+        cov_xy = sum(frame[0][c] * frame[1][c] for c in range(3))
+        cov_yy = sum(frame[1][c] * frame[1][c] for c in range(3)) + DILATION
+        inverse = 1.0 / (cov_xx * cov_yy - cov_xy * cov_xy)
+        mean_u = turn[0][0] * shift_x + turn[0][1] * shift_y + turn[0][2] * rows[2] + centre_x
+        mean_w = turn[1][0] * shift_x + turn[1][1] * shift_y + turn[1][2] * rows[2] + centre_y
+        records.append(
+            [mean_u, mean_w, cov_yy * inverse, -cov_xy * inverse, cov_xx * inverse, opacity]
+        )
+    return records
+
+
+def split_parts(value):
+    high = value.astype(jnp.bfloat16)
+    rest = value - high.astype(jnp.float32)
+    middle = rest.astype(jnp.bfloat16)
+    low = (rest - middle.astype(jnp.float32)).astype(jnp.bfloat16)
+    return jnp.concatenate([high, middle, low], axis=0)
+
+
+def chunk_of(total):
+    return 256 if total % 256 == 0 else total
+
+
+def one_hot(lists_ref, start, chunk, splats):
+    wanted = lists_ref[:, pl.ds(start, chunk)]
+    rows = lax.broadcasted_iota(jnp.int32, (splats, chunk), 0)
+    return jnp.where(rows == wanted, 1.0, 0.0).astype(jnp.bfloat16)
+
+
+def project_kernel(centre_x, centre_y, params_ref, lists_ref, camera_ref, extra_ref, out_ref, rec_ref, parts_ref):
+    splats = params_ref.shape[1]
+    total = lists_ref.shape[1]
+    turn = camera_rotation([camera_ref[:, i : i + 1] for i in range(3)])
+    rows = [params_ref[i : i + 1, :] for i in range(11)]
+    record = geometry(rows, [turn], centre_x, centre_y)[0]
+    basis = harmonics(turn[2])
+    colour = 0.5 + basis[0] * params_ref[11:14, :]
+    for i in range(1, 16):
+        colour = colour + basis[i] * params_ref[11 + 3 * i : 14 + 3 * i, :]
+    rec_ref[...] = jnp.zeros_like(rec_ref)
+    for i in range(6):
+        rec_ref[i : i + 1, :] = record[i]
+    rec_ref[6:9, :] = colour
+    parts_ref[...] = split_parts(rec_ref[...])
+    chunk = chunk_of(total)
+
+    def step(index, carry):
+        start = pl.multiple_of(index * chunk, chunk)
+        picked = jnp.dot(
+            parts_ref[...],
+            one_hot(lists_ref, start, chunk, splats),
+            preferred_element_type=jnp.float32,
+        )
+        out_ref[:, pl.ds(start, chunk)] = picked[0:16] + picked[16:32] + picked[32:48]
+        return carry
+
+    lax.fori_loop(0, total // chunk, step, 0)
+    out_ref[9:10, :] = extra_ref[...]
+
+
+def unpick_kernel(grads_ref, lists_ref, camera_ref, out_ref, acc_ref):
+    splats = out_ref.shape[1]
+    total = lists_ref.shape[1]
+    chunk = chunk_of(total)
+    acc_ref[...] = jnp.zeros_like(acc_ref)
+
+    def step(index, carry):
+        start = pl.multiple_of(index * chunk, chunk)
+        acc_ref[...] += lax.dot_general(
+            split_parts(grads_ref[:, pl.ds(start, chunk)]),
+            one_hot(lists_ref, start, chunk, splats),
+            (((1,), (1,)), ((), ())),
+            preferred_element_type=jnp.float32,
+        )
+        return carry
+
+    lax.fori_loop(0, total // chunk, step, 0)
+    out_ref[...] = acc_ref[0:16, :] + acc_ref[16:32, :] + acc_ref[32:48, :]
+    for i in range(3):
+        out_ref[9 + i : 10 + i, :] = jnp.broadcast_to(camera_ref[:, i : i + 1], (1, splats))
+
+
+def unproject_kernel(centre_x, centre_y, params_ref, grads_ref, out_ref):
+    views = grads_ref.shape[0]
+    turns = [
+        camera_rotation([grads_ref[v, 9 + i : 10 + i, 0:1] for i in range(3)]) for v in range(views)
     ]
-    cov_xx = (
-        frame[0][0] * frame[0][0] + frame[0][1] * frame[0][1] + frame[0][2] * frame[0][2] + DILATION
-    )
-    cov_xy = frame[0][0] * frame[1][0] + frame[0][1] * frame[1][1] + frame[0][2] * frame[1][2]
-    cov_yy = (
-        frame[1][0] * frame[1][0] + frame[1][1] * frame[1][1] + frame[1][2] * frame[1][2] + DILATION
-    )
-    determinant = cov_xx * cov_yy - cov_xy * cov_xy
-    shift_x = param_in[0] - centre_x
-    shift_y = param_in[1] - centre_y
-    mean_u = turn[0, 0] * shift_x + turn[0, 1] * shift_y + turn[0, 2] * param_in[2] + centre_x
-    mean_w = turn[1, 0] * shift_x + turn[1, 1] * shift_y + turn[1, 2] * param_in[2] + centre_y
-    opacity = jax.nn.sigmoid(param_in[10])
-    basis = harmonics(turn[2])
-    coeffs = param_in[11:59].reshape(16, 3, param_in.shape[1])
-    colour = 0.5 + jnp.sum(basis[:, None, None] * coeffs, axis=0)
-    record = jnp.stack(
-        [mean_u, mean_w, cov_yy / determinant, -cov_xy / determinant, cov_xx / determinant, opacity]
-    )
-    return jnp.concatenate([record, colour], axis=0)
-
-
-def make_projector(view_angles, centre_x, centre_y):
-
-    def apply(param_in):
-        return project(param_in, view_angles, centre_x, centre_y)
-
-    return apply
+    rows = [params_ref[i : i + 1, :] for i in range(11)]
+    pull = jax.vjp(lambda r: geometry(r, turns, centre_x, centre_y), rows)[1]
+    cotangents = [[grads_ref[v, i : i + 1, :] for i in range(6)] for v in range(views)]
+    for i, value in enumerate(pull(cotangents)[0]):
+        out_ref[i : i + 1, :] = value
+    bases = [harmonics(turn[2]) for turn in turns]
+    colours = [grads_ref[v, 6:9, :] for v in range(views)]
+    for i in range(16):
+        value = bases[0][i] * colours[0]
+        for v in range(1, views):
+            value = value + bases[v][i] * colours[v]
+        out_ref[11 + 3 * i : 14 + 3 * i, :] = value
+
+
+def whole_call(kernel, name, shape, scratch, *args):
+    return pl.pallas_call(
+        kernel,
+        name=name,
+        out_shape=jax.ShapeDtypeStruct(shape, jnp.float32),
+        in_specs=[pl.BlockSpec(memory_space=pltpu.VMEM)] * len(args),
+        out_specs=pl.BlockSpec(memory_space=pltpu.VMEM),
+        scratch_shapes=scratch,
+    )(*args)
 
 
 def render(gathered, grid_x, grid_y):
@@ -253,23 +313,26 @@
     block_rows = strip_rows // 8
     block_cols = width_px // 16
     height_px = strip_rows * devices
-    lists = visible[0]
-    slot_blocks = blocks[0]
+    splats = params.shape[1]
+    lists = visible[0].reshape(1, slot_total * list_length)
     live = jnp.arange(capacity, dtype=jnp.int32)[None, :] < counts[0][:, None]
-    target_ids = jnp.where(live, slot_blocks.reshape(devices, capacity), -1)
+    target_ids = jnp.where(live, blocks[0].reshape(devices, capacity), -1).astype(jnp.float32)
+    id_row = jnp.broadcast_to(target_ids[:, :, None], (devices, capacity, list_length))
     centre_x = 0.5 * width_px
     centre_y = 0.5 * height_px
-    records, pull_project = jax.vjp(make_projector(camera[0], centre_x, centre_y), params)
-
-    def sender_side(record_in):
-        picked = record_in[:, lists]
-        return picked.reshape(9, devices, capacity * list_length).transpose(1, 0, 2)
-
-    message, pull_sender = jax.vjp(sender_side, records)
-    received, recv_ids = (
-        lax.all_to_all(message, "space", split_axis=0, concat_axis=0, tiled=True),
-        lax.all_to_all(target_ids, "space", split_axis=0, concat_axis=0, tiled=True),
-    )
+    message = whole_call(
+        functools.partial(project_kernel, centre_x, centre_y),
+        "project",
+        (16, slot_total * list_length),
+        [pltpu.VMEM((16, splats), jnp.float32), pltpu.VMEM((48, splats), jnp.bfloat16)],
+        params,
+        lists,
+        camera,
+        id_row.reshape(1, slot_total * list_length),
+    )
+    message = message[0:10].reshape(10, devices, capacity * list_length).transpose(1, 0, 2)
+    received = lax.all_to_all(message, "space", split_axis=0, concat_axis=0, tiled=True)
+    recv_ids = received[:, 9].reshape(devices, capacity, list_length)[:, :, 0].astype(jnp.int32)
     own_blocks = jnp.maximum(recv_ids.reshape(devices * capacity), 0)
     grid_x, grid_y = pixel_grid(
         jnp.full(own_blocks.shape, me_index, jnp.int32), own_blocks, strip_rows, block_cols
@@ -284,25 +347,47 @@
         pieces = render(gathered, grid_x, grid_y).reshape(devices, capacity, 4, 128)
         return composite(pieces, recv_ids, depth_rank[0], background[0], block_rows, block_cols)
 
-    strip, pull_owner = jax.vjp(owner_side, received)
+    strip, pull_owner = jax.vjp(owner_side, received[:, 0:9])
     stacked = jnp.concatenate([strip, target[0]], axis=0)
-    extended = with_halo(stacked, (("space", 1),), 5)
+    extended = with_halo(stacked, (("space", 1),), 10)
     goal = extended[3:6]
-
-    def local_sum(picture):
-        return jnp.sum(pixel_terms(picture, goal, strip_rows))
-
-    own_loss, pull_terms = jax.vjp(local_sum, extended[0:3])
-    grad_extended = pull_terms(jnp.ones((), jnp.float32))[0]
-    from_below = passed_along(grad_extended[:, 0:5], "space", -1)
-    from_above = passed_along(grad_extended[:, strip_rows + 5 : strip_rows + 10], "space", 1)
-    grad_strip = grad_extended[:, 5 : strip_rows + 5]
-    grad_strip = grad_strip.at[:, strip_rows - 5 :].add(from_below).at[:, 0:5].add(from_above)
+    rows_here = strip_rows + 10
+    terms, pull_terms = jax.vjp(lambda p: pixel_terms(p, goal, rows_here), extended[0:3])
+    own_loss = jnp.sum(terms[:, 5 : 5 + strip_rows])
+    row_ids = jnp.arange(rows_here, dtype=jnp.int32) + me_index * strip_rows - 5
+    inside = ((row_ids >= 0) & (row_ids < height_px)).astype(jnp.float32)
+    ones = jnp.broadcast_to(inside[None, :, None], terms.shape)
+    grad_strip = pull_terms(ones)[0][:, 10 : 10 + strip_rows]
     grad_received = pull_owner(grad_strip)[0]
-    returned = lax.all_to_all(grad_received, "space", split_axis=0, concat_axis=0, tiled=True)
-    grad_records = pull_sender(returned)[0]
-    grad_params = lax.psum(pull_project(grad_records)[0], "view")
-    loss_sum = lax.psum(own_loss, "space")
+    loss_row = jnp.broadcast_to(own_loss, (devices, 1, capacity * list_length))
+    returned = lax.all_to_all(
+        jnp.concatenate([grad_received, loss_row], axis=1),
+        "space",
+        split_axis=0,
+        concat_axis=0,
+        tiled=True,
+    )
+    loss_sum = jnp.sum(returned[:, 9, 0])
+    grad_slots = returned.transpose(1, 0, 2).reshape(10, slot_total * list_length)
+    grad_slots = jnp.pad(grad_slots[0:9], ((0, 7), (0, 0)))
+    grad_records = whole_call(
+        unpick_kernel,
+        "unpick",
+        (16, splats),
+        [pltpu.VMEM((48, splats), jnp.float32)],
+        grad_slots,
+        lists,
+        camera,
+    )
+    every_view = lax.all_gather(grad_records, "view", axis=0, tiled=False)
+    grad_params = whole_call(
+        functools.partial(unproject_kernel, centre_x, centre_y),
+        "unproject",
+        params.shape,
+        [],
+        params,
+        every_view,
+    )
     loss_value = (loss_sum / (3.0 * height_px * width_px)).reshape(1)
     return (grad_params, strip[None], loss_value)
 

time: 246 us -> 115 us (0.47)
  between operations: 40.5 us -> 3.24 us
  other arithmetic: 61 us -> 23.9 us
  local copies, waits for them, and re-layouts: 49.4 us -> 16.5 us
  starting transfers between devices: 29.8 us -> 15.6 us
  Pallas kernels: 0 us -> 12.8 us
  waiting for transfers between devices: 30.6 us -> 19.7 us
  blocking collectives: 18.8 us -> 8.15 us
    psum x1 -> x0, blocking collectives: 18.8 us -> none  [shards(): loss_sum = lax.psum(own_loss, 'space')]
    add_any x10 -> x0, other arithmetic: 15.1 us -> none  [the longest x1 3.97 us: project(): part_z * part_z]
    unnamed x135 -> x69, local copies, waits for them, and re-layouts: 21.7 us -> 7.52 us
    pallas_call x0 -> x3, Pallas kernels: none -> 12.8 us  [whole_call(): pl.pallas_call(kernel, name=name, out_shape=jax.ShapeDtypeStruct(shape, j...]
    scatter-add x1 -> x0, other arithmetic: 12.3 us -> none  [sender_side(): picked = record_in[:, lists]]
    div x5 -> x0, other arithmetic: 11 us -> none  [the longest x1 4.81 us: project(): opacity = jax.nn.sigmoid(param_in[10])]
    psum x1 -> x0, waiting for transfers between devices: 10.8 us -> none  [shards(): grad_params = lax.psum(pull_project(grad_records)[0], 'view')]
    all_to_all x2 -> x1, starting transfers between devices: 14.1 us -> 4.68 us  [shards(): lax.all_to_all(jnp.concatenate([grad_received, loss_row], axis=1), 'space...]
  transfers between devices with their start and end apart: 8 -> 4, of which waited for: 6 -> 4; matrix products, arithmetic and copies ran while one was open for 11% -> 1% of each run, Pallas kernels for 0% -> 0%
where the time goes in v1:
time: 115 us; the launch traced here: 114 us
  other arithmetic  23.9 us (21%)
  waiting for transfers between devices  19.7 us (17%)
  local copies, waits for them, and re-layouts  16.5 us (14%)
  starting transfers between devices  15.6 us (14%)
  matrix products  14.2 us (12%)
  Pallas kernels  12.8 us (11%)
  blocking collectives  8.15 us (7%)
  between operations  3.24 us (3%)
    pallas_call x3, Pallas kernels, whole_call(): pl.pallas_call(kernel, name=name, out_shape=jax.ShapeDtypeStruct(shape, j...  12.8 us
    dot_general x3, matrix products, render(): jnp.einsum('skp,csk->scp', weights, gathered[6:9], precision=HIGHEST)  12 us
    all_gather x1, blocking collectives, shards(): every_view = lax.all_gather(grad_records, 'view', axis=0, tiled=False)  8.15 us
    unnamed x69, local copies, waits for them, and re-layouts  7.52 us
    all_to_all x1, waiting for transfers between devices, shards(): lax.all_to_all(message, 'space', split_axis=0, concat_axis=0, tiled=True)  7.32 us
    all_to_all x1, starting transfers between devices, shards(): lax.all_to_all(message, 'space', split_axis=0, concat_axis=0, tiled=True)  7.31 us
    all_to_all x1, waiting for transfers between devices, shards(): lax.all_to_all(jnp.concatenate([grad_received, loss_row], axis=1), 'space...  6.3 us
    ppermute x1, waiting for transfers between devices, with_halo(): before = lax.ppermute(last, axis, up)  5.9 us
  transfers between devices with their start and end apart: 4, of which 4 were waited for; matrix products, arithmetic and copies ran while one was open for 1% of the time, Pallas kernels for 0%

profile of v1, /device:TPU:0, one launch (start us, length us, event | category | flops | bytes accessed | tf_op | source)
XLA Modules:
  0.0 113.9 jit_solution(12949749248739057759)
XLA Ops:
  0.6 0.5 broadcast.725
  1.3 0.7 reduce.20
  2.0 0.7 copy-done.29
  2.9 0.7 reshape.318.extra_ref
  3.6 0.7 reshape_squeeze.9.lists_ref
  4.3 4.4 %project.1 = f32[16,2048]{1,0:T(8,128)} custom-call(f32[59,2048]{1,0:T(8,128)} %params_ref.3, s32[1,2048]{1,0:T(1,128)} %reshape_squeeze.9.lists_ref, f32[1,3]{1,0:T(1,128)} %camera_ref.3, f32[1,2048]{1,0:T(1,128)} %reshape.318.extra_ref), custom_call_target="tpu_custom_call" | custom-call | tf_op jit(solution)/shard_map/project/pallas_call | solution.py:221
  8.7 0.9 copy.130
  9.7 0.7 copy.173
  10.4 7.3 %all-to-all-start = ((f32[8,10,256]{2,1,0:T(8,128)}), f32[8,10,256]{2,1,0:T(8,128)S(1)}, u32[]{:S(2)}, u32[]{:S(2)}) async-start(f32[8,10,256]{2,1,0:T(8,128)} %bitcast.96), calls=%async_computation | async-start | bytes 262144 | tf_op jit(solution)/shard_map/all_to_all | solution.py:334
  17.7 7.3 %all-to-all-done = f32[8,10,256]{2,1,0:T(8,128)S(1)} async-done(((f32[8,10,256]{2,1,0:T(8,128)}), f32[8,10,256]{2,1,0:T(8,128)S(1)}, u32[]{:S(2)}, u32[]{:S(2)}) %all-to-all-start) | async-done | bytes 81952 | tf_op jit(solution)/shard_map/all_to_all | solution.py:334
  25.4 0.5 fusion.211
  26.8 1.7 %negate_log-plus-one_fusion = (f32[128,16,128]{2,1,0:T(8,128)S(1)}, f32[128,128]{1,0:T(8,128)S(1)}) fusion(f32[128,16]{1,0:T(8,128)S(1)} %bitcast.110, f32[128,16]{1,0:T(8,128)S(1)} %bitcast.115, f32[128,16]{1,0:T(8,128)S(1)} %bitcast.120, f32[128,128]{1,0:T(8,128)S(1)} %get-tuple-element.85, f32[128,16]{1,0:T(8,128)S(1)} %bitcast.125, ...), kind=kLoop, calls=%fused_computation.50 | loop fusion | flops 3915776 | bytes 1294336 | tf_op jit(solution)/shard_map/jvp()/log1p | solution.py:240
  29.0 3.7 %fusion.28 = f32[128,3,128]{2,1,0:T(4,128)S(1)} fusion(f32[3,128,16]{2,0,1:T(4,128)S(1)} %bitcast.152, f32[128,16]{1,0:T(8,128)S(1)} %bitcast.111, f32[128,16,128]{2,0,1:T(8,128)S(1)} %fusion.26, f32[128,16]{1,0:T(8,128)S(1)} %bitcast.116, f32[128,16]{1,0:T(8,128)S(1)} %bitcast.121, f32[128,128]{1,0:T(8,128)S(1)} %get-tuple-element.85, ...), kind=kOutput, calls=%fused_computation.108 | convolution fusion | flops 13631488 | bytes 1449984 | tf_op jit(solution)/shard_map/jvp(skp,csk->scp)/dot_general | solution.py:243
  32.7 0.7 convolution_bitcast_fusion
  33.5 0.6 copy-done.22
  34.2 0.7 copy-done.26
  34.8 0.5 convolution_exponential_fusion
  35.6 0.7 copy-done.28
  37.3 0.5 copy-done.21
  37.8 2.1 %collective-permute-start = (f32[6,10,512]{2,1,0:T(8,128)S(1)}, f32[6,10,512]{2,1,0:T(8,128)S(1)}, u32[]{:S(2)}, u32[]{:S(2)}) collective-permute-start(f32[6,10,512]{2,1,0:T(8,128)S(1)} %get-tuple-element.79), channel_id=1, source_target_pairs={{0,4},{4,8},{8,12},{12,16},{16,20},{20,24},{24,28},{1,5},{5,9},{9,... | collective-permute-start | bytes 368648 | tf_op jit(solution)/shard_map/ppermute | solution.py:43
  40.0 1.5 %collective-permute-start.1 = (f32[6,10,512]{2,1,0:T(8,128)S(1)}, f32[6,10,512]{2,1,0:T(8,128)S(1)}, u32[]{:S(2)}, u32[]{:S(2)}) collective-permute-start(f32[6,10,512]{2,1,0:T(8,128)S(1)} %get-tuple-element.80), channel_id=1, source_target_pairs={{4,0},{8,4},{12,8},{16,12},{20,16},{24,20},{28,24},{5,1},{9,5},{13... | collective-permute-start | bytes 368648 | tf_op jit(solution)/shard_map/ppermute | solution.py:44
  41.5 5.9 %collective-permute-done = f32[6,10,512]{2,1,0:T(8,128)S(1)} collective-permute-done((f32[6,10,512]{2,1,0:T(8,128)S(1)}, f32[6,10,512]{2,1,0:T(8,128)S(1)}, u32[]{:S(2)}, u32[]{:S(2)}) %collective-permute-start) | collective-permute-done | bytes 122912 | tf_op jit(solution)/shard_map/ppermute | solution.py:43
  47.7 0.8 add_sqrt_fusion
  48.6 0.7 fusion.89
  49.3 0.7 fusion.129
  50.0 0.7 fusion.109
  50.7 0.7 fusion.49
  51.4 0.7 fusion.69
  52.1 1.4 %fusion.209 = (f32[3,26,512]{2,1,0:T(8,128)}, f32[3,26,512]{2,1,0:T(8,128)S(1)}, f32[3,26,512]{2,1,0:T(8,128)S(1)}, f32[3,26,512]{2,1,0:T(8,128)S(1)}) fusion(f32[3,36,512]{2,1,0:T(8,128)S(1)} %fusion.129, f32[3,36,512]{2,1,0:T(8,128)S(1)} %fusion.69, f32[3,36,512]{2,1,0:T(8,128)S(1)} %fusion.49), kind=kLoop, calls=%fused_computation.431 | loop fusion | flops 2835456 | bytes 5910528 | tf_op jit(solution)/shard_map/jvp()/mul | solution.py:297
  53.5 1.2 %fusion.212 = (f32[3,26,512]{2,1,0:T(8,128)}, f32[3,26,512]{2,1,0:T(8,128)S(1)}) fusion(f32[3,26,512]{2,1,0:T(8,128)S(1)} %get-tuple-element.14, f32[3,26,512]{2,1,0:T(8,128)S(1)} %get-tuple-element.15, f32[3,36,512]{2,1,0:T(8,128)S(1)} %fusion.109, f32[3,36,512]{2,1,0:T(8,128)S(1)} %fusion.89), kind=kLoop, calls=%fused_computation.434 | loop fusion | flops 2036736 | bytes 4153344 | tf_op jit(solution)/shard_map/jvp()/mul | solution.py:299
  60.7 0.7 copy-done.23
  61.9 0.5 fusion.18
  62.6 0.5 copy-done.1
  63.6 4.4 %convolution_bitcast_fusion.1 = f32[3,128,16]{2,0,1:T(4,128)S(1)} fusion(f32[128,16]{1,0:T(8,128)S(1)} %bitcast.112, f32[128,16,128]{2,0,1:T(8,128)S(1)} %copy-done.1, f32[128,3,128]{2,0,1:T(8,128)S(1)} %split.8, f32[128,16]{1,0:T(8,128)S(1)} %bitcast.117, f32[128,16]{1,0:T(8,128)S(1)} %bitcast.122, f32[128,128]{1,0:T(8,128)S(1)} %copy-done.15, ...), kind=kOutput, calls=%fused_computation.16 | convolution fusion | flops 13631488 | bytes 1449984 | tf_op jit(solution)/shard_map/transpose(jvp(skp,csk->scp))/dot_general | solution.py:243
  68.0 4.0 %multiply_multiply_fusion = (f32[128,16,128]{2,1,0:T(8,128)S(1)}, f32[128,16,128]{2,1,0:T(8,128)S(1)}) fusion(f32[128,16]{1,0:T(8,128)S(1)} %bitcast.113, f32[128,16,128]{2,0,1:T(8,128)S(1)} %copy-done.1, f32[128,16]{1,0:T(8,128)S(1)} %bitcast.118, f32[128,16]{1,0:T(8,128)S(1)} %bitcast.123, f32[128,128]{1,0:T(8,128)S(1)} %copy-done.15, ...), kind=kOutput, calls=%fused_computation.48 | convolution fusion | flops 13893632 | bytes 3547136 | tf_op jit(solution)/shard_map/transpose(jvp(skp,csk->scp))/dot_general | solution.py:243
  72.3 5.6 %fusion.15 = (f32[128,16]{1,0:T(8,128)S(1)}, f32[128,16]{1,0:T(8,128)S(1)}, f32[128,16]{1,0:T(8,128)S(1)}, f32[128,16]{1,0:T(8,128)S(1)}, f32[128,16]{1,0:T(8,128)S(1)}, /*index=5*/f32[128,16]{1,0:T(8,128)S(1)}) fusion(f32[128,16]{1,0:T(8,128)S(1)} %bitcast.124, f32[128,128]{1,0:T(8,128)S(1)} %copy-done.15, f32[128,16]{1,0:T(8,128)S(1)} %bitcast.119, ...), kind=kLoop, calls=%fused_computation.30 | loop fusion | flops 13357056 | bytes 3440640 | tf_op jit(solution)/shard_map/transpose(jvp())/reduce_sum | solution.py:237
  77.9 0.9 pad_add_fusion
  79.3 0.6 copy-done.19
  80.3 0.7 fusion.200
  80.9 1.3 %concatenate.22.clone = f32[8,10,256]{2,1,0:T(8,128)} pad(f32[8,9,256]{2,1,0:T(8,128)S(1)} %copy.128, f32[]{:T(128)} %fusion.200), padding=0_0x0_1x0_0 | pad | bytes 155652 | tf_op jit(solution)/shard_map/concatenate | solution.py:364
  82.2 4.7 %all-to-all-start.1 = ((f32[8,10,256]{2,1,0:T(8,128)}), f32[8,10,256]{2,1,0:T(8,128)S(1)}, u32[]{:S(2)}, u32[]{:S(2)}) async-start(f32[8,10,256]{2,1,0:T(8,128)} %concatenate.22.clone), calls=%async_computation.1 | async-start | bytes 262144 | tf_op jit(solution)/shard_map/all_to_all | solution.py:363
  86.9 1.0 reshape.328
  87.9 6.3 %all-to-all-done.1 = f32[8,10,256]{2,1,0:T(8,128)S(1)} async-done(((f32[8,10,256]{2,1,0:T(8,128)}), f32[8,10,256]{2,1,0:T(8,128)S(1)}, u32[]{:S(2)}, u32[]{:S(2)}) %all-to-all-start.1) | async-done | bytes 81952 | tf_op jit(solution)/shard_map/all_to_all | solution.py:363
  94.4 0.7 pad.347.grads_ref
  95.0 5.1 %unpick.1 = f32[16,2048]{1,0:T(8,128)} custom-call(f32[16,2048]{1,0:T(8,128)} %pad.347.grads_ref, s32[1,2048]{1,0:T(1,128)} %reshape_squeeze.9.lists_ref, f32[1,3]{1,0:T(1,128)} %camera_ref.3), custom_call_target="tpu_custom_call" | custom-call | tf_op jit(solution)/shard_map/unpick/pallas_call | solution.py:221
  100.1 8.1 %all-gather = f32[64,2048]{1,0:T(8,128)} all-gather(f32[16,2048]{1,0:T(8,128)} %unpick.1), channel_id=2, replica_groups=mesh['space'=8,'view'=4] {'view'}, dimensions={0}, use_global_device_ids=true | all-gather | bytes 655360 | tf_op jit(solution)/shard_map/all_gather | solution.py:382
  108.3 3.3 %unproject.1 = f32[59,2048]{1,0:T(8,128)} custom-call(f32[59,2048]{1,0:T(8,128)} %params_ref.3, f32[4,16,2048]{2,1,0:T(8,128)} %bitcast.105), custom_call_target="tpu_custom_call" | custom-call | tf_op jit(solution)/shard_map/unproject/pallas_call | solution.py:221
  111.6 0.6 slice_reduce_fusion.2
  (133 shorter events, 12.0 us)
Async XLA Ops:
  0.6 0.7 copy-start.30
  2.0 0.7 copy-start.29
  2.8 0.7 copy-start.27
  10.4 14.7 %all-to-all-start = ((f32[8,10,256]{2,1,0:T(8,128)}), f32[8,10,256]{2,1,0:T(8,128)S(1)}, u32[]{:S(2)}, u32[]{:S(2)}) async-start(f32[8,10,256]{2,1,0:T(8,128)} %bitcast.96), calls=%async_computation | async-start | bytes 262144 | tf_op jit(solution)/shard_map/all_to_all | solution.py:334
  26.2 2.7 %copy-start.2 = (f32[1,8,16,16]{3,2,1,0:T(8,128)}, f32[1,8,16,16]{3,2,1,0:T(8,128)S(1)}, u32[]{:S(2)}) copy-start(f32[1,8,16,16]{3,2,1,0:T(8,128)S(1)} %get-tuple-element.34) | copy-start | bytes 24580
  26.2 2.7 %copy-start.4 = (f32[1,8,16,16]{3,2,1,0:T(8,128)}, f32[1,8,16,16]{3,2,1,0:T(8,128)S(1)}, u32[]{:S(2)}) copy-start(f32[1,8,16,16]{3,2,1,0:T(8,128)S(1)} %get-tuple-element.35) | copy-start | bytes 24580
  26.2 2.7 %copy-start.6 = (f32[1,8,16,16]{3,2,1,0:T(8,128)}, f32[1,8,16,16]{3,2,1,0:T(8,128)S(1)}, u32[]{:S(2)}) copy-start(f32[1,8,16,16]{3,2,1,0:T(8,128)S(1)} %get-tuple-element.36) | copy-start | bytes 24580
  26.2 2.7 %copy-start.8 = (f32[1,8,16,16]{3,2,1,0:T(8,128)}, f32[1,8,16,16]{3,2,1,0:T(8,128)S(1)}, u32[]{:S(2)}) copy-start(f32[1,8,16,16]{3,2,1,0:T(8,128)S(1)} %get-tuple-element.37) | copy-start | bytes 24580
  26.2 2.7 %copy-start.10 = (f32[1,8,16,16]{3,2,1,0:T(8,128)}, f32[1,8,16,16]{3,2,1,0:T(8,128)S(1)}, u32[]{:S(2)}) copy-start(f32[1,8,16,16]{3,2,1,0:T(8,128)S(1)} %get-tuple-element.38) | copy-start | bytes 24580
  26.2 2.7 %copy-start.12 = (f32[1,8,16,16]{3,2,1,0:T(8,128)}, f32[1,8,16,16]{3,2,1,0:T(8,128)S(1)}, u32[]{:S(2)}) copy-start(f32[1,8,16,16]{3,2,1,0:T(8,128)S(1)} %get-tuple-element.39) | copy-start | bytes 24580
  26.6 2.3 %copy-start.24 = (f32[3,8,16,16]{3,0,2,1:T(4,128)}, f32[3,8,16,16]{3,0,2,1:T(4,128)S(1)}, u32[]{:S(2)}) copy-start(f32[3,8,16,16]{3,0,2,1:T(4,128)S(1)} %copy.84) | copy-start | bytes 73732
  26.8 2.2 %copy-start.14 = (f32[128,128]{1,0:T(8,128)}, f32[128,128]{1,0:T(8,128)S(1)}, u32[]{:S(2)}) copy-start(f32[128,128]{1,0:T(8,128)S(1)} %get-tuple-element.85) | copy-start | bytes 196612
  26.8 2.2 %copy-start.16 = (f32[128,128]{1,0:T(8,128)}, f32[128,128]{1,0:T(8,128)S(1)}, u32[]{:S(2)}) copy-start(f32[128,128]{1,0:T(8,128)S(1)} %get-tuple-element.86) | copy-start | bytes 196612
  28.9 3.8 %copy-start = (f32[128,16,128]{2,0,1:T(8,128)}, f32[128,16,128]{2,0,1:T(8,128)S(1)}, u32[]{:S(2)}) copy-start(f32[128,16,128]{2,0,1:T(8,128)S(1)} %fusion.26) | copy-start | bytes 3145732
  33.5 0.6 copy-start.22
  34.2 0.7 copy-start.26
  35.6 0.7 copy-start.28
  36.9 0.9 copy-start.21
  37.8 9.5 %collective-permute-start = (f32[6,10,512]{2,1,0:T(8,128)S(1)}, f32[6,10,512]{2,1,0:T(8,128)S(1)}, u32[]{:S(2)}, u32[]{:S(2)}) collective-permute-start(f32[6,10,512]{2,1,0:T(8,128)S(1)} %get-tuple-element.79), channel_id=1, source_target_pairs={{0,4},{4,8},{8,12},{12,16},{16,20},{20,24},{24,28},{1,5},{5,9},{9,... | collective-permute-start | bytes 368648 | tf_op jit(solution)/shard_map/ppermute | solution.py:43
  40.0 7.6 %collective-permute-start.1 = (f32[6,10,512]{2,1,0:T(8,128)S(1)}, f32[6,10,512]{2,1,0:T(8,128)S(1)}, u32[]{:S(2)}, u32[]{:S(2)}) collective-permute-start(f32[6,10,512]{2,1,0:T(8,128)S(1)} %get-tuple-element.80), channel_id=1, source_target_pairs={{4,0},{8,4},{12,8},{16,12},{20,16},{24,20},{28,24},{5,1},{9,5},{13... | collective-permute-start | bytes 368648 | tf_op jit(solution)/shard_map/ppermute | solution.py:44
  60.7 0.8 copy-start.23
  61.9 1.2 %copy-start.1 = (f32[128,16,128]{2,0,1:T(8,128)S(1)}, f32[128,16,128]{2,0,1:T(8,128)}, u32[]{:S(2)}) copy-start(f32[128,16,128]{2,0,1:T(8,128)} %copy-done) | copy-start | bytes 3145732
  62.5 0.9 copy-start.15
  62.5 0.9 copy-start.17
  62.5 0.9 copy-start.3
  62.5 0.9 copy-start.5
  62.6 0.9 copy-start.7
  62.6 0.9 copy-start.9
  62.6 1.0 copy-start.11
  62.6 1.0 copy-start.13
  63.6 4.4 %copy-start.25 = (f32[3,8,16,16]{3,0,2,1:T(4,128)S(1)}, f32[3,8,16,16]{3,0,2,1:T(4,128)}, u32[]{:S(2)}) copy-start(f32[3,8,16,16]{3,0,2,1:T(4,128)} %copy-done.24) | copy-start | bytes 73732
  79.0 0.9 copy-start.19
  79.0 1.0 copy-start.20
  79.3 1.0 copy-start.18
  82.2 12.0 %all-to-all-start.1 = ((f32[8,10,256]{2,1,0:T(8,128)}), f32[8,10,256]{2,1,0:T(8,128)S(1)}, u32[]{:S(2)}, u32[]{:S(2)}) async-start(f32[8,10,256]{2,1,0:T(8,128)} %concatenate.22.clone), calls=%async_computation.1 | async-start | bytes 262144 | tf_op jit(solution)/shard_map/all_to_all | solution.py:363
